TPU v7x, 32 devices: a whole 2x2x4 slice. The times are simulated.
32 devices in a mesh: row: 4 (over x, core), col: 8 (over z, y).
Axes of the slice: x: 2, y: 2, z: 4, core: 2. Of those that a mesh axis runs over, the one named last changes fastest.
Arguments:
- blocks: float32 [256, 8, 128, 128], P(('row', 'col')), may hold values from -2 to 2
- prolong: float32 [256, 128, 128], P(('row', 'col')), may hold values from -0.5 to 0.5
- counts: int32 [256], P(('row', 'col')), may hold values from 1 to 8
- columns: int32 [256, 8], P(('row', 'col')), may hold values from 0 to 63, as said below
- aggregates: int32 [256], P(('row', 'col')), may hold values from 0 to 1
Outputs:
- coarse_operator: float32 [64, 16, 128, 128], P(('row', 'col'))
Inputs may be any that keep to these rules, and one draw needn't show every extreme that they name: Over all slots of the 8 rows of one device, the columns that fall among the rows of any one device of the slab (columns // 8 equal) take at most 2 distinct values; every device reaches 2 for some such device.
All inputs are finite; a program needn't handle non-finite values.
Results may differ from a plain program's by a relative error of at most 0.0003.
Values sent between devices are 32-bit elements; how exact they have to be, the bound alone decides.
A program may use at most 64 MiB of HBM per device.

v0:
```python
import jax
import jax.numpy as jnp
from jax import lax
from jax.sharding import PartitionSpec as P

AGD = 2
CAP = 2


def per_device(blocks, prolong, counts, columns, aggregates):
    rows_here, slots = columns.shape
    tile = blocks.shape[-1]
    peers = lax.axis_size("col")
    wide = AGD * peers
    high = lax.Precision.HIGHEST
    flat_cols = columns.reshape(-1)
    slab_agg = lax.all_gather(aggregates, "col", axis=0, tiled=True)
    col_agg = jnp.take(slab_agg, columns, axis=0)
    coarse_col = columns // rows_here * AGD + col_agg
    every_block = jnp.arange(rows_here * peers, dtype=jnp.int32)
    wanted = jnp.any(flat_cols[:, None] == every_block[None, :], axis=0)
    wanted = wanted.reshape(peers, rows_here).astype(jnp.int32)
    rank = jnp.cumsum(wanted, axis=1) - 1
    places = jnp.arange(CAP, dtype=jnp.int32)
    local_ids = jnp.arange(rows_here, dtype=jnp.int32)
    match = (wanted[:, :, None] > 0) & (rank[:, :, None] == places[None, None, :])
    valid = jnp.any(match, axis=1)
    chosen = jnp.sum(jnp.where(match, local_ids[None, :, None], 0), axis=1)
    requests = jnp.where(valid, chosen, -1)
    asked = lax.all_to_all(requests, "col", split_axis=0, concat_axis=0, tiled=True)
    found = jnp.take(prolong, jnp.clip(asked, 0, rows_here - 1).reshape(-1), axis=0)
    found = jnp.where((asked.reshape(-1) >= 0)[:, None, None], found, 0.0)
    found = found.reshape(peers, CAP, tile, tile)
    replies = lax.all_to_all(found, "col", split_axis=0, concat_axis=0, tiled=True)
    replies = replies.reshape(peers * CAP, tile, tile)
    owner = flat_cols // rows_here
    within = flat_cols % rows_here
    slot_rank = rank.reshape(-1)[owner * rows_here + within]
    picked = jnp.take(replies, owner * CAP + slot_rank, axis=0)
    picked = picked.reshape(rows_here, slots, tile, tile)
    inner = jnp.einsum("bkxy,bkyz->bkxz", blocks, picked, precision=high)
    terms = jnp.einsum("bxw,bkxz->bkwz", prolong, inner, precision=high)
    live = (jnp.arange(slots, dtype=jnp.int32)[None, :] < counts[:, None]).astype(jnp.float32)
    col_hot = (coarse_col[:, :, None] == jnp.arange(wide, dtype=jnp.int32)[None, None, :]).astype(
        jnp.float32
    ) * live[:, :, None]
    row_hot = (aggregates[:, None] == jnp.arange(AGD, dtype=jnp.int32)[None, :]).astype(jnp.float32)
    weights = (row_hot[:, None, :, None] * col_hot[:, :, None, :]).reshape(
        rows_here * slots, AGD * wide
    )
    flat_terms = terms.reshape(rows_here * slots, tile * tile)
    galerkin = jnp.dot(weights.T, flat_terms, precision=high).reshape(AGD, wide, tile, tile)
    local_most = jnp.max(jnp.sum(jnp.abs(galerkin), axis=(1, 3)))
    bound = lax.pmax(local_most, ("row", "col"))
    return galerkin / (bound + 1e-06)


def solution(mesh):
    placed = (
        P(("row", "col"), None, None, None),
        P(("row", "col"), None, None),
        P(("row", "col")),
        P(("row", "col"), None),
        P(("row", "col")),
    )
    return jax.shard_map(
        per_device,
        mesh=mesh,
        in_specs=placed,
        out_specs=P(("row", "col"), None, None, None),
        check_vma=False,
    )
```

profile of v0, /device:TPU:0, one launch (start us, length us, event | category | flops | bytes accessed | tf_op | source)
XLA Modules:
  0.0 128.0 jit_solution(14758266157524943750)
XLA Ops:
  0.0 0.8 reshape.305
  0.8 0.1 fusion.13
  1.0 0.2 reduce_window_sum.11
  1.2 0.2 select_reduce_fusion
  1.3 0.2 fusion.15
  1.5 0.7 copy.53
  2.2 7.3 %all-to-all-start = ((s32[8,1,2]{2,1,0:T(1,128)}), s32[8,1,2]{2,1,0:T(1,128)S(1)}, u32[]{:S(2)}, u32[]{:S(2)}) async-start(s32[8,1,2]{2,1,0:T(1,128)} %copy.53), calls=%async_computation | async-start | bytes 8192 | tf_op jit(solution)/shard_map/all_to_all | solution.py:30
  9.5 0.8 reshape.306
  10.3 0.7 add_select_fusion
  11.0 4.9 %all-to-all-done = s32[8,1,2]{2,1,0:T(1,128)S(1)} async-done(((s32[8,1,2]{2,1,0:T(1,128)}), s32[8,1,2]{2,1,0:T(1,128)S(1)}, u32[]{:S(2)}, u32[]{:S(2)}) %all-to-all-start) | async-done | bytes 96 | tf_op jit(solution)/shard_map/all_to_all | solution.py:30
  16.2 0.1 copy.55
  16.3 0.1 copy.57
  16.4 0.6 gather_fusion.2
  17.1 1.2 select_select_fusion
  18.2 3.6 %all-to-all-start.1 = ((f32[8,2,128,128]{3,2,1,0:T(8,128)}), f32[8,2,128,128]{3,2,1,0:T(8,128)S(1)}, u32[]{:S(2)}, u32[]{:S(2)}) async-start(f32[8,2,128,128]{3,2,1,0:T(8,128)} %select_select_fusion), calls=%async_computation.1 | async-start | bytes 2097152 | tf_op jit(solution)/shard_map/all_to_all | solution.py:34
  21.9 0.8 gather_fusion.1
  22.8 0.7 dynamic-slice
  24.2 0.2 dynamic-update-slice
  24.5 22.2 %all-reduce = s32[64]{0:T(128)S(1)} all-reduce(s32[64]{0:T(128)S(1)} %dynamic-update-slice), channel_id=1, replica_groups=mesh['row'=4,'col'=8] {'col'}, use_global_device_ids=true, to_apply=%add | all-reduce | flops 64 | bytes 512
  46.7 0.8 gather_fusion
  47.8 0.1 broadcast_multiply_fusion
  47.9 0.1 mul.65
  48.1 2.7 %gather_fusion.3 = f32[64,128,128]{2,1,0:T(8,128)} fusion(f32[16,128,128]{2,1,0:T(8,128)S(1)} %bitcast.63, s32[1024]{0:T(1024)S(1)} %pad_clamp_fusion), kind=kCustom, calls=%fused_computation.3 | custom fusion | bytes 8388864 | tf_op jit(solution)/shard_map/jit(_take)/gather | solution.py:39
  50.9 5.3 %copy.59 = f32[8,8,128,128]{2,3,1,0:T(8,128)} copy(f32[8,8,128,128]{3,2,1,0:T(8,128)} %bitcast.64) | data formatting | bytes 8388608 | tf_op jit(solution)/shard_map/jit(_take)/gather | solution.py:39
  56.2 11.4 %fusion.4 = f32[8,8,128,128]{3,2,1,0:T(8,128)S(1)} fusion(f32[8,8,128,128]{3,2,1,0:T(8,128)} %param.5, f32[8,8,128,128]{2,3,1,0:T(8,128)} %copy.59, pred[8,8]{1,0:T(8,128)(4,1)S(1)} %compare_and_fusion), kind=kOutput, calls=%fused_computation.10 | convolution fusion | flops 1611661312 | bytes 12582976 | tf_op jit(solution)/shard_map/bkxy,bkyz->bkxz/dot_general | solution.py:41
  67.7 5.1 %fusion.6 = f32[8,8,128,128]{2,3,1,0:T(8,128)} fusion(f32[8,8,128,128]{3,2,1,0:T(8,128)S(1)} %fusion.4, f32[8,128,128]{2,1,0:T(8,128)S(1)} %copy-done), kind=kOutput, calls=%fused_computation.12 | convolution fusion | flops 1610612736 | bytes 8912896 | tf_op jit(solution)/shard_map/bxw,bkxz->bkwz/dot_general | solution.py:42
  72.8 5.3 %copy.60 = f32[8,8,128,128]{3,2,1,0:T(8,128)} copy(f32[8,8,128,128]{2,3,1,0:T(8,128)} %fusion.6) | data formatting | bytes 8388608 | tf_op jit(solution)/shard_map/bxw,bkxz->bkwz/transpose | solution.py:42
  78.1 8.7 %abs_reduce_fusion = (f32[2,128]{1,0:T(2,128)S(1)}, f32[2,16,128,128]{3,1,2,0:T(8,128)S(1)}) fusion(f32[2,16,64,1]{2,1,3,0:T(8,128)S(1)} %bitcast.67, f32[8,8,128,128]{3,2,1,0:T(8,128)} %copy.60), kind=kOutput, calls=%fused_computation.13 | convolution fusion | flops 403701504 | bytes 6300672 | tf_op jit(solution)/shard_map/dot_general | solution.py:52
  86.9 0.6 reduce_max.9
  87.5 37.8 %pmax.7 = f32[]{:T(128)} all-reduce(f32[]{:T(128)} %reduce_max.9), channel_id=1, replica_groups=mesh['row'=4,'col'=8] {'row','col'}, use_global_device_ids=true, to_apply=%region_6.7 | all-reduce | flops 1 | bytes 8 | tf_op jit(solution)/shard_map/pmax | solution.py:54
  125.9 0.1 broadcast_divide_fusion
  126.1 1.9 %copy.62 = f32[2,16,128,128]{3,2,1,0:T(8,128)} copy(f32[2,16,128,128]{3,1,2,0:T(8,128)S(1)} %broadcast_divide_fusion) | data formatting | bytes 4194304 | tf_op jit(solution)/shard_map/div | solution.py:55
  (40 shorter events, 1.1 us)
Async XLA Ops:
  0.0 16.4 %copy-start = (f32[8,128,128]{2,1,0:T(8,128)S(1)}, f32[8,128,128]{2,1,0:T(8,128)}, u32[]{:S(2)}) copy-start(f32[8,128,128]{2,1,0:T(8,128)} %param.6) | copy-start | bytes 1572868
  0.0 22.8 %copy-start.4 = (u32[32]{0:T(128)S(1)}, u32[32]{0:T(128)}, u32[]{:S(2)}) copy-start(u32[32]{0:T(128)} %constant.111) | copy-start | bytes 388
  0.0 24.2 %copy-start.2 = (s32[8]{0:T(128)S(1)}, s32[8]{0:T(128)}, u32[]{:S(2)}) copy-start(s32[8]{0:T(128)} %param.9) | copy-start | bytes 100
  2.2 13.7 %all-to-all-start = ((s32[8,1,2]{2,1,0:T(1,128)}), s32[8,1,2]{2,1,0:T(1,128)S(1)}, u32[]{:S(2)}, u32[]{:S(2)}) async-start(s32[8,1,2]{2,1,0:T(1,128)} %copy.53), calls=%async_computation | async-start | bytes 8192 | tf_op jit(solution)/shard_map/all_to_all | solution.py:30
  17.0 30.6 %copy-start.3 = (s32[8]{0:T(128)S(1)}, s32[8]{0:T(128)}, u32[]{:S(2)}) copy-start(s32[8]{0:T(128)} %param.7) | copy-start | bytes 100
  17.0 30.7 %copy-start.1 = (s32[8,8]{1,0:T(8,128)S(1)}, s32[8,8]{1,0:T(8,128)}, u32[]{:S(2)}) copy-start(s32[8,8]{1,0:T(8,128)} %param.8) | copy-start | bytes 772
  18.2 29.9 %all-to-all-start.1 = ((f32[8,2,128,128]{3,2,1,0:T(8,128)}), f32[8,2,128,128]{3,2,1,0:T(8,128)S(1)}, u32[]{:S(2)}, u32[]{:S(2)}) async-start(f32[8,2,128,128]{3,2,1,0:T(8,128)} %select_select_fusion), calls=%async_computation.1 | async-start | bytes 2097152 | tf_op jit(solution)/shard_map/all_to_all | solution.py:34
where the time goes:
time: 129 us; the launch traced here: 128 us
  blocking collectives  60.1 us (47%)
  matrix products  25.3 us (20%)
  local copies, waits for them, and re-layouts  21.7 us (17%)
  starting transfers between devices  10.9 us (8%)
  waiting for transfers between devices  4.95 us (4%)
  other arithmetic  3.62 us (3%)
  between operations  1.51 us (1%)
    pmax x1, blocking collectives, per_device(): bound = lax.pmax(local_most, ('row', 'col'))  37.8 us
    unnamed x1, blocking collectives  22.2 us
    dot_general x1, matrix products, per_device(): inner = jnp.einsum('bkxy,bkyz->bkxz', blocks, picked, precision=high)  11.4 us
    dot_general x1, matrix products, per_device(): jnp.dot(weights.T, flat_terms, precision=high)  8.73 us
    gather x2, local copies, waits for them, and re-layouts, per_device(): picked = jnp.take(replies, owner * CAP + slot_rank, axis=0)  8.08 us
    all_to_all x1, starting transfers between devices, per_device(): lax.all_to_all(requests, 'col', split_axis=0, concat_axis=0, tiled=True)  7.31 us
    transpose x1, local copies, waits for them, and re-layouts, per_device(): terms = jnp.einsum('bxw,bkxz->bkwz', prolong, inner, precision=high)  5.34 us
    dot_general x1, matrix products, per_device(): terms = jnp.einsum('bxw,bkxz->bkwz', prolong, inner, precision=high)  5.1 us
  transfers between devices with their start and end apart: 2, of which 1 were waited for; matrix products, arithmetic and copies ran while one was open for 4% of the time, Pallas kernels for 0%

commit v1 on v0

v1 whole, which is shorter than its diff:
```python
import functools

import jax
import jax.numpy as jnp
from jax import lax
from jax.experimental import pallas as pl
from jax.experimental.pallas import tpu as pltpu
from jax.sharding import PartitionSpec as P

AGD = 2
CAP = 2
F32 = jnp.float32
BF16 = jnp.bfloat16
I32 = jnp.int32


def halves(x):
    high = x.astype(BF16)
    return high, (x - high.astype(F32)).astype(BF16)


def dot(a, b):
    return jnp.dot(a, b, preferred_element_type=F32)


def kernel(
    n, m, blocks_ref, prolong_ref, cols_v, agg_v, cols_s, agg_s, counts_s,
    out_ref, bound_ref,
    blocks, prolong, partial, table, sent, got, cols_all, agg_all, rowsum, peak, peaks_col,
    peak2, peaks_row, table_s,
    block_sem, prolong_sem, table_sem, cols_send, cols_recv, agg_send, agg_recv,
    tile_send, tile_recv, pc_send, pc_recv, pr_send, pr_recv,
):
    rows, slots = cols_v.shape
    tile = prolong.shape[-1]
    none = rows * slots
    me = lax.axis_index("col")
    my_row = lax.axis_index("row")

    load_prolong = pltpu.make_async_copy(prolong_ref, prolong, prolong_sem)
    load_prolong.start()

    def load_block(i):
        return pltpu.make_async_copy(blocks_ref.at[i], blocks.at[i], block_sem.at[i])

    @pl.loop(0, rows)
    def _(i):
        load_block(i).start()

    def across(off):
        return lax.rem(me + off, n)

    def below(off):
        return lax.rem(my_row + off, m)

    barrier = pltpu.get_barrier_semaphore()

    @pl.loop(1, n)
    def _(off):
        pl.semaphore_signal(barrier, inc=1, device_id={"col": across(off)})

    @pl.loop(1, m)
    def _(off):
        pl.semaphore_signal(barrier, inc=1, device_id={"row": below(off)})

    pl.semaphore_wait(barrier, n + m - 2)

    def far_first(t):
        return n // 2 + (lax.rem(t, 2) * 2 - 1) * (t // 2)

    def send_cols(to, slot):
        return pltpu.make_async_remote_copy(
            cols_v, cols_all.at[slot], cols_send.at[to], cols_recv.at[slot], device_id={"col": to}
        )

    def send_agg(to, slot):
        return pltpu.make_async_remote_copy(
            agg_v, agg_all.at[slot], agg_send.at[to], agg_recv.at[slot], device_id={"col": to}
        )

    @pl.loop(1, n)
    def _(t):
        to = across(far_first(t))
        send_cols(to, me).start()
        send_agg(to, me).start()

    sub = lax.broadcasted_iota(I32, (8, 128), 0)
    lane = lax.broadcasted_iota(I32, (8, 128), 1)
    keys = jnp.full((8, 128), -1, I32)
    for i in range(rows):
        for k in range(slots):
            here = (sub == i) & (lane == k)
            keys = jnp.where(here, cols_s[i, k] * AGD + agg_s[i], keys)
    order = sub * slots + lane

    def scan_keys(i, carry):
        prev, low, high = carry
        for k in range(slots):
            col = cols_s[i, k]
            s = i * slots + k
            owner, within = col // rows, lax.rem(col, rows)
            key = jnp.where(k < counts_s[i], col * AGD + agg_s[i], -2)
            prev = jnp.where((keys == key) & (order > s), s, prev)
            low = jnp.where(lane == owner, jnp.minimum(low, within), low)
            high = jnp.where(lane == owner, jnp.maximum(high, within), high)
        return prev, low, high

    prev, low, high = lax.fori_loop(
        0, rows, scan_keys,
        (jnp.full((8, 128), none, I32), jnp.full((8, 128), rows - 1, I32), jnp.zeros((8, 128), I32)),
    )
    wanted = jnp.where(lax.rem(sub, 2) == 0, low, jnp.where(high > low, high, -1))

    def scan_last(i, last):
        for k in range(slots):
            col = cols_s[i, k]
            owner, within = col // rows, lax.rem(col, rows)
            row = jnp.where(k < counts_s[i], agg_s[i], -1)
            hit = (lane == owner) & (sub // 2 == row) & (wanted == within)
            last = jnp.where(hit, i * slots + k, last)
        return last

    last = lax.fori_loop(0, rows, scan_last, jnp.full((8, 128), none, I32))
    table[0:8, :] = prev
    table[8:16, :] = last
    table[16:24, :] = jnp.where(sub == 0, low, high)
    to_scalars = pltpu.make_async_copy(table, table_s, table_sem)
    to_scalars.start()
    partial[none] = jnp.zeros((tile, tile), F32)
    agg_all[me] = agg_v[...]
    to_scalars.wait()

    load_prolong.wait()
    got[me, 0] = prolong[table_s[16, me]]
    got[me, 1] = prolong[table_s[17, me]]

    def send_tiles(to, slot):
        return pltpu.make_async_remote_copy(
            sent.at[to], got.at[slot], tile_send.at[to], tile_recv.at[slot], device_id={"col": to}
        )

    def reply(t, _):
        to = across(far_first(t))
        send_cols(to, to).wait_recv()
        asked = cols_all[to]
        mine = asked // rows == me
        within = lax.rem(asked, rows)
        sent[to, 0] = prolong[jnp.min(jnp.where(mine, within, rows - 1))]
        sent[to, 1] = prolong[jnp.max(jnp.where(mine, within, 0))]
        send_tiles(to, me).start()
        return 0

    lax.fori_loop(1, n, reply, 0)

    def first_product(i, _):
        load_block(i).wait()
        ph, pw = halves(prolong[i].T)
        lhs = jnp.concatenate([ph, pw, ph], axis=1)
        for k in range(0, slots, 2):
            ah, aw = halves(blocks[i, k])
            bh, bw = halves(blocks[i, k + 1])
            highs = jnp.concatenate([ah, bh], axis=1)
            rhs = jnp.concatenate([highs, highs, jnp.concatenate([aw, bw], axis=1)], axis=0)
            both = dot(lhs, rhs)
            s = i * slots + k
            partial[s] = both[:, :tile] + partial[table_s[i, k]]
            partial[s + 1] = both[:, tile:] + partial[table_s[i, k + 1]]
        return 0

    lax.fori_loop(0, rows, first_product, 0)

    rowsum[...] = jnp.zeros_like(rowsum)
    spot = lax.broadcasted_iota(I32, agg_v.shape, 1)

    def second_product(owner):
        lhs = jnp.concatenate(
            [
                jnp.concatenate([partial[table_s[8 + c * CAP + r, owner]] for r in range(CAP)], axis=1)
                for c in range(AGD)
            ],
            axis=0,
        )
        ids = agg_all[owner]
        right = []
        for r in range(CAP):
            one = jnp.max(jnp.where(spot == table_s[16 + r, owner], ids, 0)).astype(F32)
            p = got[owner, r]
            right.append(jnp.concatenate([p * (1.0 - one), p * one], axis=1))
        rhs = jnp.concatenate(right, axis=0)
        lh, lw = halves(lhs)
        rh, rw = halves(rhs)
        prod = dot(lh, rh) + dot(lh, rw) + dot(lw, rh)
        size = jnp.abs(prod)
        rowsum[...] += size[:, :tile] + size[:, tile:]
        for c in range(AGD):
            for a in range(AGD):
                out_ref[c, owner * AGD + a] = prod[
                    c * tile : (c + 1) * tile, a * tile : (a + 1) * tile
                ]

    second_product(me)

    def collect(t, _):
        owner = lax.rem(me - far_first(t) + n, n)
        send_agg(owner, owner).wait_recv()
        send_tiles(owner, owner).wait_recv()
        second_product(owner)
        return 0

    lax.fori_loop(1, n, collect, 0)

    most = jnp.max(jnp.sum(rowsum[...], axis=1, keepdims=True), axis=0, keepdims=True)
    peak[...] = jnp.broadcast_to(most, peak.shape)
    peaks_col[me] = jnp.broadcast_to(most, peak.shape)

    def send_peak(to, slot):
        return pltpu.make_async_remote_copy(
            peak, peaks_col.at[slot], pc_send.at[to], pc_recv.at[slot], device_id={"col": to}
        )

    def send_peak2(to, slot):
        return pltpu.make_async_remote_copy(
            peak2, peaks_row.at[slot], pr_send.at[to], pr_recv.at[slot], device_id={"row": to}
        )

    @pl.loop(1, n)
    def _(t):
        send_peak(across(far_first(t)), me).start()

    @pl.loop(1, n)
    def _(off):
        to = across(off)
        send_cols(to, me).wait_send()
        send_agg(to, me).wait_send()
        send_tiles(to, me).wait_send()

    @pl.loop(1, n)
    def _(off):
        send_peak(across(off), across(off)).wait_recv()

    over = jnp.max(peaks_col[...], axis=0)
    peak2[...] = over
    peaks_row[my_row] = over

    @pl.loop(1, m)
    def _(off):
        send_peak2(below(off), my_row).start()

    @pl.loop(1, m)
    def _(off):
        send_peak2(below(off), below(off)).wait_recv()

    bound_ref[...] = jnp.max(peaks_row[...], axis=0)

    @pl.loop(1, n)
    def _(off):
        send_peak(across(off), me).wait_send()

    @pl.loop(1, m)
    def _(off):
        send_peak2(below(off), my_row).wait_send()


def per_device(blocks, prolong, counts, columns, aggregates):
    rows, slots, tile, _ = blocks.shape
    n, m = lax.axis_size("col"), lax.axis_size("row")
    agg_row = aggregates.reshape(1, rows)
    dma = pltpu.SemaphoreType.DMA
    vmem = pl.BlockSpec(memory_space=pltpu.VMEM)
    smem = pl.BlockSpec(memory_space=pltpu.SMEM)
    anywhere = pl.BlockSpec(memory_space=pl.ANY)
    galerkin, bound = pl.pallas_call(
        functools.partial(kernel, n, m),
        name="galerkin",
        out_shape=(
            jax.ShapeDtypeStruct((AGD, AGD * n, tile, tile), F32),
            jax.ShapeDtypeStruct((8, 128), F32),
        ),
        in_specs=[anywhere, anywhere, vmem, vmem, smem, smem, smem],
        out_specs=(vmem, vmem),
        scratch_shapes=[
            pltpu.VMEM((rows, slots, tile, tile), F32),
            pltpu.VMEM((rows, tile, tile), F32),
            pltpu.VMEM((rows * slots + 1, tile, tile), F32),
            pltpu.VMEM((24, 128), I32),
            pltpu.VMEM((n, CAP, tile, tile), F32),
            pltpu.VMEM((n, CAP, tile, tile), F32),
            pltpu.VMEM((n, rows, slots), I32),
            pltpu.VMEM((n, 1, rows), I32),
            pltpu.VMEM((AGD * tile, tile), F32),
            pltpu.VMEM((8, 128), F32),
            pltpu.VMEM((n, 8, 128), F32),
            pltpu.VMEM((8, 128), F32),
            pltpu.VMEM((m, 8, 128), F32),
            pltpu.SMEM((24, 128), I32),
            dma((rows,)),
            dma,
            dma,
        ]
        + [dma((n,)) for _ in range(8)]
        + [dma((m,)) for _ in range(2)],
        compiler_params=pltpu.CompilerParams(
            collective_id=0, has_side_effects=True, vmem_limit_bytes=48 * 1024 * 1024
        ),
    )(blocks, prolong, columns, agg_row, columns, aggregates, counts)
    return galerkin / (bound[0, 0] + 1e-06)


def solution(mesh):
    placed = (
        P(("row", "col"), None, None, None),
        P(("row", "col"), None, None),
        P(("row", "col")),
        P(("row", "col"), None),
        P(("row", "col")),
    )
    return jax.shard_map(
        per_device,
        mesh=mesh,
        in_specs=placed,
        out_specs=P(("row", "col"), None, None, None),
        check_vma=False,
    )
```

time: 129 us -> 47.8 us (0.37)
  blocking collectives: 60.1 us -> 0 us
  Pallas kernels: 0 us -> 41.8 us
  matrix products: 25.3 us -> 0 us
  local copies, waits for them, and re-layouts: 21.7 us -> 3.55 us
  starting transfers between devices: 10.9 us -> 0 us
  waiting for transfers between devices: 4.95 us -> 0 us
  other arithmetic: 3.62 us -> 1.54 us
    pallas_call x0 -> x1, Pallas kernels: none -> 41.8 us  [per_device(): pl.pallas_call(functools.partial(kernel, n, m), name='galerkin', out_shap...]
    pmax x1 -> x0, blocking collectives: 37.8 us -> none  [per_device(): bound = lax.pmax(local_most, ('row', 'col'))]
    dot_general x3 -> x0, matrix products: 25.3 us -> none  [the longest x1 11.4 us: per_device(): inner = jnp.einsum('bkxy,bkyz->bkxz', blocks, picked, precision=high)]
    unnamed x1 -> x0, blocking collectives: 22.2 us -> none
    all_to_all x2 -> x0, starting transfers between devices: 10.9 us -> none  [the longest x1 7.31 us: per_device(): lax.all_to_all(requests, 'col', split_axis=0, concat_axis=0, tiled=True)]
    gather x7 -> x0, local copies, waits for them, and re-layouts: 10.4 us -> none  [the longest x2 8.08 us: per_device(): picked = jnp.take(replies, owner * CAP + slot_rank, axis=0)]
    transpose x1 -> x0, local copies, waits for them, and re-layouts: 5.34 us -> none  [per_device(): terms = jnp.einsum('bxw,bkxz->bkwz', prolong, inner, precision=high)]
    all_to_all x2 -> x0, waiting for transfers between devices: 4.95 us -> none  [the longest x1 4.95 us: per_device(): lax.all_to_all(requests, 'col', split_axis=0, concat_axis=0, tiled=True)]
  transfers between devices with their start and end apart: 2 -> 0, of which waited for: 1 -> 0; matrix products, arithmetic and copies ran while one was open for 4% -> 0% of each run, Pallas kernels for 0% -> 0%
where the time goes in v1:
time: 47.8 us; the launch traced here: 47.6 us
  Pallas kernels  41.8 us (87%)
  local copies, waits for them, and re-layouts  3.55 us (7%)
  other arithmetic  1.54 us (3%)
  between operations  0.67 us (1%)
    pallas_call x1, Pallas kernels, per_device(): pl.pallas_call(functools.partial(kernel, n, m), name='galerkin', out_shap...  41.8 us
    unnamed x8, local copies, waits for them, and re-layouts  3.04 us
    div x1, other arithmetic, per_device(): return galerkin / (bound[0, 0] + 1e-06)  1.54 us

profile of v1, /device:TPU:0, one launch (start us, length us, event | category | flops | bytes accessed | tf_op | source)
XLA Modules:
  0.0 47.6 jit_solution(12341067495295030034)
XLA Ops:
  0.0 0.0 copy-start
  0.0 1.0 %copy-done = f32[8,128,128]{2,1,0:T(8,128)S(1)} copy-done((f32[8,128,128]{2,1,0:T(8,128)S(1)}, f32[8,128,128]{2,1,0:T(8,128)}, u32[]{:S(2)}) %copy-start) | copy-done | bytes 524312
  1.0 0.0 copy-start.1
  1.0 0.7 %copy-done.1 = s32[8,8]{1,0:T(8,128)S(1)} copy-done((s32[8,8]{1,0:T(8,128)S(1)}, s32[8,8]{1,0:T(8,128)}, u32[]{:S(2)}) %copy-start.1) | copy-done | bytes 280
  1.7 0.0 copy-start.2
  1.7 0.7 %copy-done.2 = s32[8]{0:T(128)S(1)} copy-done((s32[8]{0:T(128)S(1)}, s32[8]{0:T(128)}, u32[]{:S(2)}) %copy-start.2) | copy-done | bytes 56
  2.4 0.0 copy-start.3
  2.4 0.7 %copy-done.3 = s32[8]{0:T(128)S(1)} copy-done((s32[8]{0:T(128)S(1)}, s32[8]{0:T(128)}, u32[]{:S(2)}) %copy-start.3) | copy-done | bytes 56
  3.0 41.8 %galerkin.1 = (f32[2,16,128,128]{3,2,1,0:T(8,128)S(1)}, f32[8,128]{1,0:T(8,128)S(1)}) custom-call(f32[8,8,128,128]{3,2,1,0:T(8,128)} %blocks_ref.1, f32[8,128,128]{2,1,0:T(8,128)S(1)} %copy-done, s32[8,8]{1,0:T(8,128)S(1)} %copy-done.1, s32[1,8]{1,0:T(1,128)S(1)} %bitcast.2, s32[8,8]{1,0:T(8,128)S(1)} %copy-done.1, s32[8]{0:T(128)S(1)} %copy-done.2, ...), custom_call_target="tpu_custom_call" | custom-call | tf_op jit(solution)/shard_map/galerkin/pallas_call | solution.py:272
  44.9 0.5 %slice.3 = f32[1,1]{1,0:T(1,128)} slice(f32[8,128]{1,0:T(8,128)S(1)} %get-tuple-element.8), slice={[0:1], [0:1]} | slice | bytes 8 | tf_op jit(solution)/shard_map/slice | solution.py:306
  46.0 1.5 %broadcast_divide_fusion = f32[2,16,128,128]{3,2,1,0:T(8,128)} fusion(f32[2,16,128,128]{3,2,1,0:T(8,128)S(1)} %get-tuple-element.7, f32[]{:T(128)} %bitcast.1), kind=kLoop, calls=%fused_computation | loop fusion | flops 524288 | bytes 4194308 | tf_op jit(solution)/shard_map/div | solution.py:306
Async XLA Ops:
  0.0 1.0 %copy-start = (f32[8,128,128]{2,1,0:T(8,128)S(1)}, f32[8,128,128]{2,1,0:T(8,128)}, u32[]{:S(2)}) copy-start(f32[8,128,128]{2,1,0:T(8,128)} %prolong_ref.1) | copy-start | bytes 1572868
  1.0 0.7 %copy-start.1 = (s32[8,8]{1,0:T(8,128)S(1)}, s32[8,8]{1,0:T(8,128)}, u32[]{:S(2)}) copy-start(s32[8,8]{1,0:T(8,128)} %cols_s.1) | copy-start | bytes 772
  1.7 0.7 %copy-start.2 = (s32[8]{0:T(128)S(1)}, s32[8]{0:T(128)}, u32[]{:S(2)}) copy-start(s32[8]{0:T(128)} %agg_s.1) | copy-start | bytes 100
  2.4 0.7 %copy-start.3 = (s32[8]{0:T(128)S(1)}, s32[8]{0:T(128)}, u32[]{:S(2)}) copy-start(s32[8]{0:T(128)} %counts_s.1) | copy-start | bytes 100

commit v2 on v1

--- a/solution.py
+++ b/solution.py
@@ -24,8 +24,9 @@
 
 
 def kernel(
-    n, m, blocks_ref, prolong_ref, cols_v, agg_v, cols_s, agg_s, counts_s,
+    n, m, blocks_ref, prolong_ref, cols_ref, agg_ref, counts_ref,
     out_ref, bound_ref,
+    cols_v, agg_v, cols_s, agg_s, counts_s, small_sem,
     blocks, prolong, partial, table, sent, got, cols_all, agg_all, rowsum, peak, peaks_col,
     peak2, peaks_row, table_s,
     block_sem, prolong_sem, table_sem, cols_send, cols_recv, agg_send, agg_recv,
@@ -38,6 +39,20 @@
     my_row = lax.axis_index("row")
 
     load_prolong = pltpu.make_async_copy(prolong_ref, prolong, prolong_sem)
+    small = [
+        pltpu.make_async_copy(src, dst, small_sem.at[at])
+        for at, (src, dst) in enumerate(
+            (
+                (cols_ref, cols_v),
+                (agg_ref, agg_v),
+                (cols_ref, cols_s),
+                (agg_ref, agg_s),
+                (counts_ref, counts_s),
+            )
+        )
+    ]
+    for copy in small:
+        copy.start()
     load_prolong.start()
 
     def load_block(i):
@@ -63,6 +78,8 @@
     def _(off):
         pl.semaphore_signal(barrier, inc=1, device_id={"row": below(off)})
 
+    for copy in small:
+        copy.wait()
     pl.semaphore_wait(barrier, n + m - 2)
 
     def far_first(t):
@@ -90,7 +107,7 @@
     for i in range(rows):
         for k in range(slots):
             here = (sub == i) & (lane == k)
-            keys = jnp.where(here, cols_s[i, k] * AGD + agg_s[i], keys)
+            keys = jnp.where(here, cols_s[i, k] * AGD + agg_s[0, i], keys)
     order = sub * slots + lane
 
     def scan_keys(i, carry):
@@ -99,7 +116,7 @@
             col = cols_s[i, k]
             s = i * slots + k
             owner, within = col // rows, lax.rem(col, rows)
-            key = jnp.where(k < counts_s[i], col * AGD + agg_s[i], -2)
+            key = jnp.where(k < counts_s[0, i], col * AGD + agg_s[0, i], -2)
             prev = jnp.where((keys == key) & (order > s), s, prev)
             low = jnp.where(lane == owner, jnp.minimum(low, within), low)
             high = jnp.where(lane == owner, jnp.maximum(high, within), high)
@@ -115,7 +132,7 @@
         for k in range(slots):
             col = cols_s[i, k]
             owner, within = col // rows, lax.rem(col, rows)
-            row = jnp.where(k < counts_s[i], agg_s[i], -1)
+            row = jnp.where(k < counts_s[0, i], agg_s[0, i], -1)
             hit = (lane == owner) & (sub // 2 == row) & (wanted == within)
             last = jnp.where(hit, i * slots + k, last)
         return last
@@ -250,7 +267,7 @@
     def _(off):
         send_peak2(below(off), below(off)).wait_recv()
 
-    bound_ref[...] = jnp.max(peaks_row[...], axis=0)
+    bound_ref[...] = jnp.broadcast_to(jnp.max(peaks_row[...], axis=0)[:1, :1], bound_ref.shape)
 
     @pl.loop(1, n)
     def _(off):
@@ -267,18 +284,23 @@
     agg_row = aggregates.reshape(1, rows)
     dma = pltpu.SemaphoreType.DMA
     vmem = pl.BlockSpec(memory_space=pltpu.VMEM)
-    smem = pl.BlockSpec(memory_space=pltpu.SMEM)
-    anywhere = pl.BlockSpec(memory_space=pl.ANY)
+    hbm = pl.BlockSpec(memory_space=pltpu.HBM)
     galerkin, bound = pl.pallas_call(
         functools.partial(kernel, n, m),
         name="galerkin",
         out_shape=(
             jax.ShapeDtypeStruct((AGD, AGD * n, tile, tile), F32),
-            jax.ShapeDtypeStruct((8, 128), F32),
+            jax.ShapeDtypeStruct((tile, tile), F32),
         ),
-        in_specs=[anywhere, anywhere, vmem, vmem, smem, smem, smem],
+        in_specs=[hbm] * 5,
         out_specs=(vmem, vmem),
         scratch_shapes=[
+            pltpu.VMEM((rows, slots), I32),
+            pltpu.VMEM((1, rows), I32),
+            pltpu.SMEM((rows, slots), I32),
+            pltpu.SMEM((1, rows), I32),
+            pltpu.SMEM((1, rows), I32),
+            dma((5,)),
             pltpu.VMEM((rows, slots, tile, tile), F32),
             pltpu.VMEM((rows, tile, tile), F32),
             pltpu.VMEM((rows * slots + 1, tile, tile), F32),
@@ -302,8 +324,8 @@
         compiler_params=pltpu.CompilerParams(
             collective_id=0, has_side_effects=True, vmem_limit_bytes=48 * 1024 * 1024
         ),
-    )(blocks, prolong, columns, agg_row, columns, aggregates, counts)
-    return galerkin / (bound[0, 0] + 1e-06)
+    )(*(pltpu.with_memory_space_constraint(x, pltpu.HBM) for x in (blocks, prolong, columns, agg_row, counts.reshape(1, rows))))
+    return galerkin / (bound + 1e-06)
 
 
 def solution(mesh):

time: 47.8 us -> 43.1 us (0.902)
  local copies, waits for them, and re-layouts: 3.55 us -> 0 us
  between operations: 0.67 us -> 0.02 us
  Pallas kernels: 41.8 us -> 41.3 us
    unnamed x8 -> x0, local copies, waits for them, and re-layouts: 3.04 us -> none
    pallas_call x1, Pallas kernels: 41.8 us -> 41.3 us  [per_device(): pl.pallas_call(functools.partial(kernel, n, m), name='galerkin', out_shap...]
    slice x1 -> x0, local copies, waits for them, and re-layouts: 0.51 us -> none  [per_device(): return galerkin / (bound[0, 0] + 1e-06)]
where the time goes in v2:
time: 43.1 us; the launch traced here: 42.9 us
  Pallas kernels  41.3 us (96%)
  other arithmetic  1.63 us (4%)
    pallas_call x1, Pallas kernels, per_device(): pl.pallas_call(functools.partial(kernel, n, m), name='galerkin', out_shap...  41.3 us
    div x1, other arithmetic, per_device(): return galerkin / (bound + 1e-06)  1.62 us

profile of v2, /device:TPU:0, one launch (start us, length us, event | category | flops | bytes accessed | tf_op | source)
XLA Modules:
  0.0 42.9 jit_solution(3511137179720204883)
XLA Ops:
  0.0 41.3 %galerkin.1 = (f32[2,16,128,128]{3,2,1,0:T(8,128)S(1)}, f32[128,128]{1,0:T(8,128)S(1)}) custom-call(f32[8,8,128,128]{3,2,1,0:T(8,128)} %blocks_ref.1, f32[8,128,128]{2,1,0:T(8,128)} %prolong_ref.1, s32[8,8]{1,0:T(8,128)} %cols_ref.1, s32[1,8]{1,0:T(1,128)} %bitcast.2, s32[1,8]{1,0:T(1,128)} %bitcast.3), custom_call_target="tpu_custom_call" | custom-call | tf_op jit(solution)/shard_map/galerkin/pallas_call | solution.py:288
  41.3 1.6 %broadcast_divide_fusion = f32[2,16,128,128]{3,2,1,0:T(8,128)} fusion(f32[2,16,128,128]{3,2,1,0:T(8,128)S(1)} %get-tuple-element.7, f32[128,128]{1,0:T(8,128)S(1)} %broadcast_add_fusion), kind=kLoop, calls=%fused_computation | loop fusion | flops 524288 | bytes 4259840 | tf_op jit(solution)/shard_map/div | solution.py:328
  (1 shorter events, 0.0 us)

commit v3 on v2

--- a/solution.py
+++ b/solution.py
@@ -99,7 +99,10 @@
     def _(t):
         to = across(far_first(t))
         send_cols(to, me).start()
-        send_agg(to, me).start()
+
+    @pl.loop(1, n)
+    def _(t):
+        send_agg(across(far_first(t)), me).start()
 
     sub = lax.broadcasted_iota(I32, (8, 128), 0)
     lane = lax.broadcasted_iota(I32, (8, 128), 1)
@@ -267,7 +270,9 @@
     def _(off):
         send_peak2(below(off), below(off)).wait_recv()
 
-    bound_ref[...] = jnp.broadcast_to(jnp.max(peaks_row[...], axis=0)[:1, :1], bound_ref.shape)
+    bound_ref[...] = jnp.broadcast_to(
+        jnp.max(peaks_row[...], axis=0)[:1, :1] + 1e-06, bound_ref.shape
+    )
 
     @pl.loop(1, n)
     def _(off):
@@ -325,7 +330,7 @@
             collective_id=0, has_side_effects=True, vmem_limit_bytes=48 * 1024 * 1024
         ),
     )(*(pltpu.with_memory_space_constraint(x, pltpu.HBM) for x in (blocks, prolong, columns, agg_row, counts.reshape(1, rows))))
-    return galerkin / (bound + 1e-06)
+    return galerkin / bound
 
 
 def solution(mesh):

time: 43.1 us -> 43.1 us (level)
  no operation moved by 1% of the time
where the time goes in v3:
time: 43.1 us; the launch traced here: 42.9 us
  Pallas kernels  41.3 us (96%)
  other arithmetic  1.62 us (4%)
    pallas_call x1, Pallas kernels, per_device(): pl.pallas_call(functools.partial(kernel, n, m), name='galerkin', out_shap...  41.3 us
    div x1, other arithmetic, per_device(): return galerkin / bound  1.62 us

profile of v3, /device:TPU:0, one launch (start us, length us, event | category | flops | bytes accessed | tf_op | source)
XLA Modules:
  0.0 42.9 jit_solution(12592485697069654479)
XLA Ops:
  0.0 41.3 %galerkin.1 = (f32[2,16,128,128]{3,2,1,0:T(8,128)S(1)}, f32[128,128]{1,0:T(8,128)S(1)}) custom-call(f32[8,8,128,128]{3,2,1,0:T(8,128)} %blocks_ref.1, f32[8,128,128]{2,1,0:T(8,128)} %prolong_ref.1, s32[8,8]{1,0:T(8,128)} %cols_ref.1, s32[1,8]{1,0:T(1,128)} %bitcast.2, s32[1,8]{1,0:T(1,128)} %bitcast.3), custom_call_target="tpu_custom_call" | custom-call | tf_op jit(solution)/shard_map/galerkin/pallas_call | solution.py:293
  41.3 1.6 %broadcast_divide_fusion = f32[2,16,128,128]{3,2,1,0:T(8,128)} fusion(f32[2,16,128,128]{3,2,1,0:T(8,128)S(1)} %get-tuple-element.7, f32[128,128]{1,0:T(8,128)S(1)} %get-tuple-element.8), kind=kLoop, calls=%fused_computation | loop fusion | flops 524288 | bytes 4259840 | tf_op jit(solution)/shard_map/div | solution.py:333
